TPU v7x, 32 devices: a whole 2x2x4 slice. The times are simulated.
32 devices in a mesh: leaf: 16 (over z, y, x), sub: 2 (over core).
Axes of the slice: x: 2, y: 2, z: 4, core: 2. Of those that a mesh axis runs over, the one named last changes fastest.
Arguments:
- probes: float32 [64, 32768], P(None, ('leaf', 'sub')), may hold values from -600 to 600
- points: float32 [3, 32768], P(None, ('leaf', 'sub')), may hold values from -4 to 4
- leaf_order: int32 [32768], P(('leaf', 'sub')), may hold values from 0 to 1023, as said below
- near_list: int32 [64, 4], P(('leaf', 'sub')), may hold values from 0 to 63, as said below
- far_leaf_list: int32 [64, 2], P(('leaf', 'sub')), may hold values from 0 to 63, as said below
- far_chip_list: int32 [16, 8], P('leaf'), may hold values from -1 to 15, as said below
- leaf_basis: float32 [64, 512, 256], P(('leaf', 'sub')), may hold values from -0.25 to 0.25
- transfer: float32 [64, 256, 256], P(('leaf', 'sub')), may hold values from -0.1875 to 0.1875
- far_leaf_blocks: float32 [128, 256, 256], P(('leaf', 'sub')), may hold values from -0.25 to 0.25
- far_chip_blocks: float32 [128, 256, 256], P('leaf'), may hold values from -0.125 to 0.125
Outputs:
- result: float32 [64, 32768], P(None, ('leaf', 'sub'))
Inputs may be any that keep to these rules, and one draw needn't show every extreme that they name: `leaf_order`: each device's block of 1024 consecutive entries is a permutation of 0 to 1023. `near_list`: row l lists 4 distinct leaves, l among them, all held by the devices l // 2 - 1 to l // 2 + 1 of the joined axis leaf+sub, counted around the cycle. `far_leaf_list`: row l lists the 2 leaves of those same three devices that row l of near_list leaves out. `far_chip_list`: row k lists distinct chip clusters at cycle distance 2 to 5 from k, one to 8 of them, the used entries first and -1 in the rest; some row uses all 8.
All inputs are finite; a program needn't handle non-finite values.
Results may differ from a plain program's by a relative error of at most 0.0003.
Values sent between devices are 32-bit elements; how exact they have to be, the bound alone decides.
No kernel may reach another device: no remote copies, remote signals or barrier semaphores. Data moves between devices by JAX's collectives and lax.ppermute only.
A program may use at most 64 MiB of HBM per device.

v0:
```python
import jax
import jax.numpy as jnp
from jax import lax
from jax.sharding import PartitionSpec as P

CHIP_SPAN = 4
highest = lax.Precision.HIGHEST
inverse_width = 0.5 / (0.15 * 0.15)
epsilon = 1e-06


def from_behind(block, axis, distance):
    devices = range(lax.axis_size(axis))
    route = [((i - distance) % len(devices), i) for i in devices]
    return lax.ppermute(block, axis, route)


def kernel_tiles(source_points, target_points):
    spread = source_points[0] - target_points[0]
    distance = spread * spread
    for coord_axis in (1, 2):
        spread = source_points[coord_axis] - target_points[coord_axis]
        distance = distance + spread * spread
    return jnp.exp(-inverse_width * distance)


def leaf_window(values):
    pieces = []
    for offset in (1, 0, -1):
        if offset == 0:
            pieces.append(values)
        else:
            pieces.append(from_behind(values, ("leaf", "sub"), offset))
    first_device = lax.axis_index(("leaf", "sub")) - 1
    return (jnp.concatenate(pieces, 1), first_device)


def couple_chips(stacked, slot_place, used_count, far_chip_blocks):

    def add_slot(slot_index, running):
        source = stacked[slot_place[slot_index]]
        return running + jnp.dot(
            source,
            far_chip_blocks[slot_index],
            precision=highest,
            preferred_element_type=jnp.float32,
        )

    start_value = jnp.zeros((stacked.shape[1], stacked.shape[2]), jnp.float32)
    return lax.fori_loop(0, used_count, add_slot, start_value)


def chip_level(upward, far_chip_list, far_chip_blocks):
    chip_count = lax.axis_size("leaf")
    chip_index = lax.axis_index("leaf")
    slot_ids = far_chip_list[0]
    used_count = jnp.sum((slot_ids >= 0).astype(jnp.int32))
    offsets = jnp.mod(slot_ids - chip_index, chip_count)
    slot_place = jnp.where(
        offsets <= CHIP_SPAN + 1, offsets - 2, CHIP_SPAN + chip_count - offsets - 2
    )
    slot_place = jnp.clip(slot_place, 0, 2 * CHIP_SPAN - 1)
    shift_list = [-distance for distance in range(2, CHIP_SPAN + 2)] + [
        distance for distance in range(2, CHIP_SPAN + 2)
    ]
    halves = lax.psum_scatter(upward, "sub", scatter_dimension=0, tiled=True)
    pieces = [from_behind(halves, "leaf", offset) for offset in shift_list]
    coupled_half = couple_chips(jnp.stack(pieces), slot_place, used_count, far_chip_blocks)
    coupled = lax.all_gather(coupled_half, "sub", axis=0, tiled=True)
    return coupled


def apply_matrix(
    sorted_values,
    kernels,
    near_index,
    leaf_basis,
    transfer,
    far_leaf_list,
    far_leaf_blocks,
    far_chip_list,
    far_chip_blocks,
    leaf_total,
):
    columns = sorted_values.shape[0]
    leaf_count, leaf_size, rank_size = leaf_basis.shape
    value_window, window_start = leaf_window(sorted_values)
    window_tiles = value_window.reshape(columns, -1, leaf_size)
    source_values = jnp.take(window_tiles, near_index, axis=1)
    near_part = jnp.einsum("clnp,lnpq->clq", source_values, kernels, precision=highest)
    own_tiles = sorted_values.reshape(columns, leaf_count, leaf_size)
    coefficients = jnp.einsum("clp,lpr->lcr", own_tiles, leaf_basis, precision=highest)
    pieces = []
    for offset in (1, 0, -1):
        if offset == 0:
            pieces.append(coefficients)
        else:
            pieces.append(from_behind(coefficients, ("leaf", "sub"), offset))
    coeff_stack = jnp.concatenate(pieces, 0)
    device_index = lax.axis_index(("leaf", "sub"))
    far_index = jnp.mod(far_leaf_list - (device_index - 1) * leaf_count, leaf_total)
    far_sources = jnp.take(coeff_stack, far_index.reshape(-1), axis=0).reshape(
        leaf_count, -1, columns, rank_size
    )
    leaf_blocks = far_leaf_blocks.reshape(leaf_count, -1, rank_size, rank_size)
    local_far = jnp.einsum("ljcr,ljrs->lcs", far_sources, leaf_blocks, precision=highest)
    upward = jnp.einsum("lcr,lrs->cs", coefficients, transfer, precision=highest)
    chip_part = chip_level(upward, far_chip_list, far_chip_blocks)
    downward = local_far + jnp.einsum("cs,lrs->lcr", chip_part, transfer, precision=highest)
    far_part = jnp.einsum("lcr,lpr->clp", downward, leaf_basis, precision=highest)
    return (near_part + far_part).reshape(columns, leaf_count * leaf_size)


def on_device(
    probes,
    points,
    leaf_order,
    near_list,
    far_leaf_list,
    far_chip_list,
    leaf_basis,
    transfer,
    far_leaf_blocks,
    far_chip_blocks,
):
    leaf_count, leaf_size, rank_size = leaf_basis.shape
    leaf_total = leaf_count * lax.axis_size(("leaf", "sub"))
    point_total = probes.shape[1] * lax.axis_size(("leaf", "sub"))
    sorted_probes = probes[:, leaf_order]
    sorted_points = points[:, leaf_order]
    point_window, first_device = leaf_window(sorted_points)
    near_index = jnp.mod(near_list - first_device * leaf_count, leaf_total)
    point_tiles = point_window.reshape(3, -1, leaf_size)
    source_points = jnp.take(point_tiles, near_index, axis=1)
    target_points = sorted_points.reshape(3, leaf_count, leaf_size)
    kernels = kernel_tiles(source_points[..., :, None], target_points[:, :, None, None, :])
    first_pass = apply_matrix(
        sorted_probes,
        kernels,
        near_index,
        leaf_basis,
        transfer,
        far_leaf_list,
        far_leaf_blocks,
        far_chip_list,
        far_chip_blocks,
        leaf_total,
    )
    squares = lax.psum(jnp.sum(first_pass * first_pass, axis=1), ("leaf", "sub"))
    column_scale = lax.rsqrt(squares / point_total + epsilon)
    second = apply_matrix(
        first_pass * column_scale[:, None],
        kernels,
        near_index,
        leaf_basis,
        transfer,
        far_leaf_list,
        far_leaf_blocks,
        far_chip_list,
        far_chip_blocks,
        leaf_total,
    )
    return jnp.zeros_like(second).at[:, leaf_order].set(second)


def solution(mesh):
    return jax.shard_map(
        on_device,
        mesh=mesh,
        in_specs=(
            P(None, ("leaf", "sub")),
            P(None, ("leaf", "sub")),
            P(("leaf", "sub")),
            P(("leaf", "sub"), None),
            P(("leaf", "sub"), None),
            P("leaf", None),
            P(("leaf", "sub"), None, None),
            P(("leaf", "sub"), None, None),
            P(("leaf", "sub"), None, None),
            P("leaf", None, None),
        ),
        out_specs=P(None, ("leaf", "sub")),
        check_vma=False,
    )
```

profile of v0, /device:TPU:5, one launch (start us, length us, event | category | flops | bytes accessed | tf_op | source)
XLA Modules:
  0.0 316.3 jit_solution(15570008534534858504)
XLA Ops:
  9.1 4.0 %gather_fusion.2 = f32[1024,64]{1,0:T(8,128)} fusion(f32[64,1024]{0,1:T(8,128)S(1)} %copy.43, s32[1024]{0:T(1024)S(1)} %get-tuple-element.107), kind=kCustom, calls=%fused_computation.6 | custom fusion | bytes 528384 | tf_op jit(solution)/shard_map/gather | solution.py:129
  13.1 2.1 fusion.58
  17.1 1.8 copy.39
  18.9 3.8 %gather_fusion = f32[1024,3]{1,0:T(8,128)S(1)} fusion(f32[3,1024]{0,1:T(8,128)} %copy.39, s32[1024]{0:T(1024)S(1)} %get-tuple-element.107), kind=kCustom, calls=%fused_computation.4 | custom fusion | bytes 28672 | tf_op jit(solution)/shard_map/gather | solution.py:130
  37.8 1.8 copy.42
  45.1 5.9 %collective-permute-start.6 = (f32[32,256]{1,0:T(8,128)}, f32[32,256]{1,0:T(8,128)S(1)}, u32[]{:S(2)}, u32[]{:S(2)}) collective-permute-start(f32[32,256]{1,0:T(8,128)} %reduce-scatter.3.cloned.1.call-done), channel_id=1, source_target_pairs={{4,0},{6,2},{8,4},{10,6},{12,8},{14,10},{16,12},{18,14},{20,16},{2... | collective-permute-start | bytes 98312 | tf_op jit(solution)/shard_map/ppermute | solution.py:15
  51.8 1.8 collective-permute-start.13
  54.9 10.9 %collective-permute-start.7 = (f32[32,256]{1,0:T(8,128)}, f32[32,256]{1,0:T(8,128)S(1)}, u32[]{:S(2)}, u32[]{:S(2)}) collective-permute-start(f32[32,256]{1,0:T(8,128)} %reduce-scatter.3.cloned.1.call-done), channel_id=1, source_target_pairs={{6,0},{8,2},{10,4},{12,6},{14,8},{16,10},{18,12},{20,14},{22,16},{... | collective-permute-start | bytes 98312 | tf_op jit(solution)/shard_map/ppermute | solution.py:15
  67.3 3.2 %collective-permute-done.8 = f32[32,256]{1,0:T(8,128)S(1)} collective-permute-done((f32[32,256]{1,0:T(8,128)}, f32[32,256]{1,0:T(8,128)S(1)}, u32[]{:S(2)}, u32[]{:S(2)}) %collective-permute-start.8) | collective-permute-done | bytes 32800 | tf_op jit(solution)/shard_map/ppermute | solution.py:15
  70.6 5.1 %collective-permute-start.9 = (f32[32,256]{1,0:T(8,128)}, f32[32,256]{1,0:T(8,128)S(1)}, u32[]{:S(2)}, u32[]{:S(2)}) collective-permute-start(f32[32,256]{1,0:T(8,128)} %reduce-scatter.3.cloned.1.call-done), channel_id=1, source_target_pairs={{10,0},{12,2},{14,4},{16,6},{18,8},{20,10},{22,12},{24,14},{26,16}... | collective-permute-start | bytes 98312 | tf_op jit(solution)/shard_map/ppermute | solution.py:15
  77.0 1.8 collective-permute-start.10
  80.3 2.5 collective-permute-start.11
  82.8 3.7 %collective-permute-done.11 = f32[32,256]{1,0:T(8,128)S(1)} collective-permute-done((f32[32,256]{1,0:T(8,128)}, f32[32,256]{1,0:T(8,128)S(1)}, u32[]{:S(2)}, u32[]{:S(2)}) %collective-permute-start.11) | collective-permute-done | bytes 32800 | tf_op jit(solution)/shard_map/ppermute | solution.py:15
  87.2 38.6 %while.20 = (s32[]{:T(128)}, f32[32,256]{1,0:T(8,128)S(1)}, s32[]{:T(128)}, s32[8]{0:T(128)}, f32[8,32,256]{2,1,0:T(8,128)}, /*index=5*/f32[8,256,256]{2,1,0:T(8,128)}, s32[]{:T(128)}, s32[]{:T(128)}, s32[]{:T(128)}) while((s32[]{:T(128)}, f32[32,256]{1,0:T(8,128)S(1)}, s32[]{:T(128)}, s32[8]{0:T(128)}, f32[8,32,256]{2,1,0:T(8,128)}, ...), condition=%wide.region_3.6_spmd, body=%wide.region_2.5_spmd.sunk | while | flops 25174024 | bytes 360637 | solution.py:50
  125.8 3.8 %all_gather.6 = f32[64,256]{1,0:T(8,128)S(1)} all-gather(f32[32,256]{1,0:T(8,128)S(1)} %get-tuple-element.73), channel_id=1, replica_groups=mesh['leaf'=16,'sub'=2] {'sub'}, dimensions={0}, use_global_device_ids=true | all-gather | bytes 98304 | tf_op jit(solution)/shard_map/all_gather | solution.py:69
  130.3 2.5 pad_maximum_fusion
  132.7 3.6 %gather_fusion.3 = f32[8,64,512]{1,2,0:T(8,128)} fusion(f32[64,6,512]{0,2,1:T(8,128)} %bitcast.168, s32[1024]{0:T(1024)} %pad_clamp_fusion.1), kind=kCustom, calls=%fused_computation.clone | custom fusion | bytes 2097184 | tf_op jit(solution)/shard_map/jit(_take)/gather | solution.py:89
  136.3 3.2 %copy.44 = f32[8,64,512]{2,1,0:T(8,128)} copy(f32[8,64,512]{1,2,0:T(8,128)} %gather_fusion.3) | data formatting | bytes 2097152 | tf_op jit(solution)/shard_map/jit(_take)/gather | solution.py:89
  139.5 9.7 %fusion.26 = f32[64,2,512]{2,0,1:T(8,128)S(1)} fusion(f32[2,512]{1,0:T(2,128)S(1)} %copy-done.13, f32[2,4,512]{2,1,0:T(4,128)S(1)} %copy-done.5, f32[2,512]{1,0:T(2,128)S(1)} %copy-done.11, f32[2,4,512]{2,1,0:T(4,128)S(1)} %copy-done.7, f32[2,512]{1,0:T(2,128)S(1)} %copy-done.9, f32[2,4,512]{2,1,0:T(4,128)S(1)} %bitcast.184, ...), kind=kOutput, calls=%fused_computation.38 | convolution fusion | flops 1629749248 | bytes 1372168 | tf_op jit(solution)/shard_map/clnp,lnpq->clq/dot_general | solution.py:90
  150.5 39.2 %psum.7 = f32[64]{0:T(128)S(1)} all-reduce(f32[64]{0:T(128)S(1)} %get-tuple-element.109), channel_id=1, replica_groups=mesh['leaf'=16,'sub'=2] {'leaf','sub'}, use_global_device_ids=true, to_apply=%region_5.8 | all-reduce | flops 64 | bytes 512 | tf_op jit(solution)/shard_map/psum | solution.py:149
  199.2 10.4 %reduce-scatter.5.cloned.1.call-done = f32[32,256]{1,0:T(8,128)} async-done(((f32[64,256]{1,0:T(8,128)}), f32[32,256]{1,0:T(8,128)}) %reduce-scatter.5.cloned.1.call-update) | async-done | bytes 32784 | tf_op jit(solution)/shard_map/reduce_scatter | solution.py:66
  210.3 2.4 collective-permute-start.25
  214.0 5.3 %collective-permute-start.19 = (f32[32,256]{1,0:T(8,128)}, f32[32,256]{1,0:T(8,128)S(1)}, u32[]{:S(2)}, u32[]{:S(2)}) collective-permute-start(f32[32,256]{1,0:T(8,128)} %reduce-scatter.5.cloned.1.call-done), channel_id=1, source_target_pairs={{6,0},{8,2},{10,4},{12,6},{14,8},{16,10},{18,12},{20,14},{22,16},{... | collective-permute-start | bytes 98312 | tf_op jit(solution)/shard_map/ppermute | solution.py:15
  220.6 4.5 %collective-permute-start.20 = (f32[32,256]{1,0:T(8,128)}, f32[32,256]{1,0:T(8,128)S(1)}, u32[]{:S(2)}, u32[]{:S(2)}) collective-permute-start(f32[32,256]{1,0:T(8,128)} %reduce-scatter.5.cloned.1.call-done), channel_id=1, source_target_pairs={{8,0},{10,2},{12,4},{14,6},{16,8},{18,10},{20,12},{22,14},{24,16},... | collective-permute-start | bytes 98312 | tf_op jit(solution)/shard_map/ppermute | solution.py:15
  226.4 2.6 collective-permute-start.21
  230.4 1.8 collective-permute-start.22
  233.5 2.4 collective-permute-start.23
  235.9 4.2 %collective-permute-done.23 = f32[32,256]{1,0:T(8,128)S(1)} collective-permute-done((f32[32,256]{1,0:T(8,128)}, f32[32,256]{1,0:T(8,128)S(1)}, u32[]{:S(2)}, u32[]{:S(2)}) %collective-permute-start.23) | collective-permute-done | bytes 32800 | tf_op jit(solution)/shard_map/ppermute | solution.py:15
  240.2 42.2 %while.21 = (s32[]{:T(128)}, f32[32,256]{1,0:T(8,128)S(1)}, s32[]{:T(128)}, s32[8]{0:T(128)}, f32[8,32,256]{2,1,0:T(8,128)S(1)}, /*index=5*/f32[8,256,256]{2,1,0:T(8,128)}, s32[]{:T(128)}, s32[]{:T(128)}, s32[]{:T(128)}) while((s32[]{:T(128)}, f32[32,256]{1,0:T(8,128)S(1)}, s32[]{:T(128)}, s32[8]{0:T(128)}, f32[8,32,256]{2,1,0:T(8,128)S(1)}, ...), condition=%wide.region_8.11_spmd, body=%wide.region_7.10_spmd.sunk | while | flops 25174024 | bytes 360637 | solution.py:50
  282.4 8.1 %all_gather.7 = f32[64,256]{1,0:T(8,128)S(1)} all-gather(f32[32,256]{1,0:T(8,128)S(1)} %get-tuple-element.74), channel_id=1, replica_groups=mesh['leaf'=16,'sub'=2] {'sub'}, dimensions={0}, use_global_device_ids=true | all-gather | bytes 98304 | tf_op jit(solution)/shard_map/all_gather | solution.py:69
  294.2 9.7 %fusion.27 = f32[64,2,512]{2,0,1:T(8,128)S(1)} fusion(f32[2,512]{1,0:T(2,128)S(1)} %copy-done.14, f32[2,4,512]{2,1,0:T(4,128)S(1)} %copy-done.6, f32[2,512]{1,0:T(2,128)S(1)} %copy-done.12, f32[2,4,512]{2,1,0:T(4,128)S(1)} %copy-done.8, f32[2,512]{1,0:T(2,128)S(1)} %copy-done.10, f32[2,4,512]{2,1,0:T(4,128)S(1)} %bitcast.185, ...), kind=kOutput, calls=%fused_computation.39 | convolution fusion | flops 1629749248 | bytes 1372168 | tf_op jit(solution)/shard_map/clnp,lnpq->clq/dot_general | solution.py:90
  305.2 3.3 %scatter_custom_fusion = f32[64,1024]{0,1:T(8,128)S(1)} fusion(s32[1024]{0:T(1024)} %get-tuple-element.108, f32[1024,64]{1,0:T(8,128)S(1)} %copy.49, f32[]{:T(128)} %constant.109.clone.1), kind=kCustom, calls=%fused_computation.71 | custom fusion | bytes 262656 | tf_op jit(solution)/shard_map/scatter | solution.py:163
  (182 shorter events, 96.3 us)
Async XLA Ops:
  6.5 44.5 %copy-start = (f32[4,256,256]{2,1,0:T(8,128)S(1)}, f32[4,256,256]{2,1,0:T(8,128)}, u32[]{:S(2)}) copy-start(f32[4,256,256]{2,1,0:T(8,128)} %param.26) | copy-start | bytes 3145732
  6.5 38.6 %reduce-scatter.3.cloned.1.call-start = ((), (), s32[]{:S(2)}) async-start(), calls=%async_computation.2 | async-start | bytes 98304 | tf_op jit(solution)/shard_map/reduce_scatter | solution.py:66
  13.1 16.4 %copy-start.19 = (s32[1,8]{1,0:T(1,128)S(1)}, s32[1,8]{1,0:T(1,128)}, u32[]{:S(2)}) copy-start(s32[1,8]{1,0:T(1,128)} %param.23) | copy-start | bytes 100
  13.1 17.0 %copy-start.17 = (s32[2,4]{1,0:T(2,128)S(1)}, s32[2,4]{1,0:T(2,128)}, u32[]{:S(2)}) copy-start(s32[2,4]{1,0:T(2,128)} %param.21) | copy-start | bytes 100
  15.2 28.4 %collective-permute-start.5 = (f32[2,64,256]{2,1,0:T(8,128)S(1)}, f32[2,64,256]{2,1,0:T(8,128)S(1)}, u32[]{:S(2)}, u32[]{:S(2)}) collective-permute-start(f32[2,64,256]{2,1,0:T(8,128)S(1)} %fusion.58), channel_id=1, source_target_pairs={{1,0},{2,1},{3,2},{4,3},{5,4},{6,5},{7,6},{8,7},{9,8},{10,9},{11,1... | collective-permute-start | bytes 393224 | tf_op jit(solution)/shard_map/ppermute | solution.py:15
  15.9 27.7 %collective-permute-start.4 = (f32[2,64,256]{2,1,0:T(8,128)S(1)}, f32[2,64,256]{2,1,0:T(8,128)S(1)}, u32[]{:S(2)}, u32[]{:S(2)}) collective-permute-start(f32[2,64,256]{2,1,0:T(8,128)S(1)} %fusion.58), channel_id=1, source_target_pairs={{31,0},{0,1},{1,2},{2,3},{3,4},{4,5},{5,6},{6,7},{7,8},{8,9},{9,10... | collective-permute-start | bytes 393224 | tf_op jit(solution)/shard_map/ppermute | solution.py:15
  22.7 13.9 %collective-permute-start.1 = (f32[3,1024]{0,1:T(8,128)S(1)}, f32[3,1024]{0,1:T(8,128)}, u32[]{:S(2)}, u32[]{:S(2)}) collective-permute-start(f32[3,1024]{0,1:T(8,128)S(1)} %bitcast.164), channel_id=1, source_target_pairs={{1,0},{2,1},{3,2},{4,3},{5,4},{6,5},{7,6},{8,7},{9,8},{10,9},{11,1... | collective-permute-start | bytes 36872 | tf_op jit(solution)/shard_map/ppermute | solution.py:15
  22.8 16.8 %collective-permute-start = (f32[3,1024]{0,1:T(8,128)S(1)}, f32[3,1024]{0,1:T(8,128)}, u32[]{:S(2)}, u32[]{:S(2)}) collective-permute-start(f32[3,1024]{0,1:T(8,128)S(1)} %bitcast.165), channel_id=1, source_target_pairs={{31,0},{0,1},{1,2},{2,3},{3,4},{4,5},{5,6},{6,7},{7,8},{8,9},{9,10... | collective-permute-start | bytes 36872 | tf_op jit(solution)/shard_map/ppermute | solution.py:15
  25.6 184.0 %reduce-scatter.5.cloned.1.call-start = ((), (), s32[]{:S(2)}) async-start(), calls=%async_computation.3 | async-start | bytes 98304 | tf_op jit(solution)/shard_map/reduce_scatter | solution.py:66
  25.6 104.6 %collective-permute-start.3 = (f32[64,1024]{0,1:T(8,128)}, f32[64,1024]{0,1:T(8,128)}, u32[]{:S(2)}, u32[]{:S(2)}) collective-permute-start(f32[64,1024]{0,1:T(8,128)} %bitcast.171), channel_id=1, source_target_pairs={{1,0},{2,1},{3,2},{4,3},{5,4},{6,5},{7,6},{8,7},{9,8},{10,9},{11,1... | collective-permute-start | bytes 786440 | tf_op jit(solution)/shard_map/ppermute | solution.py:15
  36.6 93.6 %collective-permute-start.2 = (f32[64,1024]{0,1:T(8,128)}, f32[64,1024]{0,1:T(8,128)}, u32[]{:S(2)}, u32[]{:S(2)}) collective-permute-start(f32[64,1024]{0,1:T(8,128)} %bitcast.172), channel_id=1, source_target_pairs={{31,0},{0,1},{1,2},{2,3},{3,4},{4,5},{5,6},{6,7},{7,8},{8,9},{9,10... | collective-permute-start | bytes 786440 | tf_op jit(solution)/shard_map/ppermute | solution.py:15
  45.1 9.7 %collective-permute-start.6 = (f32[32,256]{1,0:T(8,128)}, f32[32,256]{1,0:T(8,128)S(1)}, u32[]{:S(2)}, u32[]{:S(2)}) collective-permute-start(f32[32,256]{1,0:T(8,128)} %reduce-scatter.3.cloned.1.call-done), channel_id=1, source_target_pairs={{4,0},{6,2},{8,4},{10,6},{12,8},{14,10},{16,12},{18,14},{20,16},{2... | collective-permute-start | bytes 98312 | tf_op jit(solution)/shard_map/ppermute | solution.py:15
  51.8 78.5 %copy-start.3 = (f32[1024,64]{1,0:T(8,128)S(1)}, f32[1024,64]{1,0:T(8,128)}, u32[]{:S(2)}) copy-start(f32[1024,64]{1,0:T(8,128)} %gather_fusion.2) | copy-start | bytes 786436
  51.8 34.6 %collective-permute-start.13 = (f32[32,256]{1,0:T(8,128)}, f32[32,256]{1,0:T(8,128)S(1)}, u32[]{:S(2)}, u32[]{:S(2)}) collective-permute-start(f32[32,256]{1,0:T(8,128)} %reduce-scatter.3.cloned.1.call-done), channel_id=1, source_target_pairs={{22,0},{24,2},{26,4},{28,6},{30,8},{0,10},{2,12},{4,14},{6,16},{8,... | collective-permute-start | bytes 98312 | tf_op jit(solution)/shard_map/ppermute | solution.py:15
  53.6 32.9 %collective-permute-start.12 = (f32[32,256]{1,0:T(8,128)}, f32[32,256]{1,0:T(8,128)S(1)}, u32[]{:S(2)}, u32[]{:S(2)}) collective-permute-start(f32[32,256]{1,0:T(8,128)} %reduce-scatter.3.cloned.1.call-done), channel_id=1, source_target_pairs={{24,0},{26,2},{28,4},{30,6},{0,8},{2,10},{4,12},{6,14},{8,16},{10,... | collective-permute-start | bytes 98312 | tf_op jit(solution)/shard_map/ppermute | solution.py:15
  54.9 12.3 %collective-permute-start.7 = (f32[32,256]{1,0:T(8,128)}, f32[32,256]{1,0:T(8,128)S(1)}, u32[]{:S(2)}, u32[]{:S(2)}) collective-permute-start(f32[32,256]{1,0:T(8,128)} %reduce-scatter.3.cloned.1.call-done), channel_id=1, source_target_pairs={{6,0},{8,2},{10,4},{12,6},{14,8},{16,10},{18,12},{20,14},{22,16},{... | collective-permute-start | bytes 98312 | tf_op jit(solution)/shard_map/ppermute | solution.py:15
  67.1 3.4 %collective-permute-start.8 = (f32[32,256]{1,0:T(8,128)}, f32[32,256]{1,0:T(8,128)S(1)}, u32[]{:S(2)}, u32[]{:S(2)}) collective-permute-start(f32[32,256]{1,0:T(8,128)} %reduce-scatter.3.cloned.1.call-done), channel_id=1, source_target_pairs={{8,0},{10,2},{12,4},{14,6},{16,8},{18,10},{20,12},{22,14},{24,16},... | collective-permute-start | bytes 98312 | tf_op jit(solution)/shard_map/ppermute | solution.py:15
  70.6 6.4 %collective-permute-start.9 = (f32[32,256]{1,0:T(8,128)}, f32[32,256]{1,0:T(8,128)S(1)}, u32[]{:S(2)}, u32[]{:S(2)}) collective-permute-start(f32[32,256]{1,0:T(8,128)} %reduce-scatter.3.cloned.1.call-done), channel_id=1, source_target_pairs={{10,0},{12,2},{14,4},{16,6},{18,8},{20,10},{22,12},{24,14},{26,16}... | collective-permute-start | bytes 98312 | tf_op jit(solution)/shard_map/ppermute | solution.py:15
  77.0 3.3 %collective-permute-start.10 = (f32[32,256]{1,0:T(8,128)}, f32[32,256]{1,0:T(8,128)S(1)}, u32[]{:S(2)}, u32[]{:S(2)}) collective-permute-start(f32[32,256]{1,0:T(8,128)} %reduce-scatter.3.cloned.1.call-done), channel_id=1, source_target_pairs={{28,0},{30,2},{0,4},{2,6},{4,8},{6,10},{8,12},{10,14},{12,16},{14,... | collective-permute-start | bytes 98312 | tf_op jit(solution)/shard_map/ppermute | solution.py:15
  80.3 6.1 %collective-permute-start.11 = (f32[32,256]{1,0:T(8,128)}, f32[32,256]{1,0:T(8,128)S(1)}, u32[]{:S(2)}, u32[]{:S(2)}) collective-permute-start(f32[32,256]{1,0:T(8,128)} %reduce-scatter.3.cloned.1.call-done), channel_id=1, source_target_pairs={{26,0},{28,2},{30,4},{0,6},{2,8},{4,10},{6,12},{8,14},{10,16},{12,... | collective-permute-start | bytes 98312 | tf_op jit(solution)/shard_map/ppermute | solution.py:15
  190.5 6.3 %collective-permute-start.17 = (f32[2,64,256]{2,1,0:T(8,128)S(1)}, f32[2,64,256]{2,1,0:T(8,128)S(1)}, u32[]{:S(2)}, u32[]{:S(2)}) collective-permute-start(f32[2,64,256]{2,1,0:T(8,128)S(1)} %fusion.41), channel_id=1, source_target_pairs={{1,0},{2,1},{3,2},{4,3},{5,4},{6,5},{7,6},{8,7},{9,8},{10,9},{11,1... | collective-permute-start | bytes 393224 | tf_op jit(solution)/shard_map/ppermute | solution.py:15
  191.7 5.1 %collective-permute-start.16 = (f32[2,64,256]{2,1,0:T(8,128)S(1)}, f32[2,64,256]{2,1,0:T(8,128)}, u32[]{:S(2)}, u32[]{:S(2)}) collective-permute-start(f32[2,64,256]{2,1,0:T(8,128)S(1)} %fusion.41), channel_id=1, source_target_pairs={{31,0},{0,1},{1,2},{2,3},{3,4},{4,5},{5,6},{6,7},{7,8},{8,9},{9,10... | collective-permute-start | bytes 393224 | tf_op jit(solution)/shard_map/ppermute | solution.py:15
  194.0 97.1 %collective-permute-start.15 = (f32[64,1024]{1,0:T(8,128)}, f32[64,1024]{1,0:T(8,128)}, u32[]{:S(2)}, u32[]{:S(2)}) collective-permute-start(f32[64,1024]{1,0:T(8,128)} %broadcast_multiply_fusion), channel_id=1, source_target_pairs={{1,0},{2,1},{3,2},{4,3},{5,4},{6,5},{7,6},{8,7},{9,8},{10,9},{11,1... | collective-permute-start | bytes 786440 | tf_op jit(solution)/shard_map/ppermute | solution.py:15
  194.0 97.1 %collective-permute-start.14 = (f32[64,1024]{1,0:T(8,128)}, f32[64,1024]{1,0:T(8,128)}, u32[]{:S(2)}, u32[]{:S(2)}) collective-permute-start(f32[64,1024]{1,0:T(8,128)} %broadcast_multiply_fusion), channel_id=1, source_target_pairs={{31,0},{0,1},{1,2},{2,3},{3,4},{4,5},{5,6},{6,7},{7,8},{8,9},{9,10... | collective-permute-start | bytes 786440 | tf_op jit(solution)/shard_map/ppermute | solution.py:15
  209.6 4.4 %collective-permute-start.18 = (f32[32,256]{1,0:T(8,128)}, f32[32,256]{1,0:T(8,128)S(1)}, u32[]{:S(2)}, u32[]{:S(2)}) collective-permute-start(f32[32,256]{1,0:T(8,128)} %reduce-scatter.5.cloned.1.call-done), channel_id=1, source_target_pairs={{4,0},{6,2},{8,4},{10,6},{12,8},{14,10},{16,12},{18,14},{20,16},{2... | collective-permute-start | bytes 98312 | tf_op jit(solution)/shard_map/ppermute | solution.py:15
  210.3 29.8 %collective-permute-start.25 = (f32[32,256]{1,0:T(8,128)}, f32[32,256]{1,0:T(8,128)S(1)}, u32[]{:S(2)}, u32[]{:S(2)}) collective-permute-start(f32[32,256]{1,0:T(8,128)} %reduce-scatter.5.cloned.1.call-done), channel_id=1, source_target_pairs={{22,0},{24,2},{26,4},{28,6},{30,8},{0,10},{2,12},{4,14},{6,16},{8,... | collective-permute-start | bytes 98312 | tf_op jit(solution)/shard_map/ppermute | solution.py:15
  212.8 27.4 %collective-permute-start.24 = (f32[32,256]{1,0:T(8,128)}, f32[32,256]{1,0:T(8,128)S(1)}, u32[]{:S(2)}, u32[]{:S(2)}) collective-permute-start(f32[32,256]{1,0:T(8,128)} %reduce-scatter.5.cloned.1.call-done), channel_id=1, source_target_pairs={{24,0},{26,2},{28,4},{30,6},{0,8},{2,10},{4,12},{6,14},{8,16},{10,... | collective-permute-start | bytes 98312 | tf_op jit(solution)/shard_map/ppermute | solution.py:15
  214.0 6.6 %collective-permute-start.19 = (f32[32,256]{1,0:T(8,128)}, f32[32,256]{1,0:T(8,128)S(1)}, u32[]{:S(2)}, u32[]{:S(2)}) collective-permute-start(f32[32,256]{1,0:T(8,128)} %reduce-scatter.5.cloned.1.call-done), channel_id=1, source_target_pairs={{6,0},{8,2},{10,4},{12,6},{14,8},{16,10},{18,12},{20,14},{22,16},{... | collective-permute-start | bytes 98312 | tf_op jit(solution)/shard_map/ppermute | solution.py:15
  220.6 5.8 %collective-permute-start.20 = (f32[32,256]{1,0:T(8,128)}, f32[32,256]{1,0:T(8,128)S(1)}, u32[]{:S(2)}, u32[]{:S(2)}) collective-permute-start(f32[32,256]{1,0:T(8,128)} %reduce-scatter.5.cloned.1.call-done), channel_id=1, source_target_pairs={{8,0},{10,2},{12,4},{14,6},{16,8},{18,10},{20,12},{22,14},{24,16},... | collective-permute-start | bytes 98312 | tf_op jit(solution)/shard_map/ppermute | solution.py:15
  226.4 4.0 %collective-permute-start.21 = (f32[32,256]{1,0:T(8,128)}, f32[32,256]{1,0:T(8,128)S(1)}, u32[]{:S(2)}, u32[]{:S(2)}) collective-permute-start(f32[32,256]{1,0:T(8,128)} %reduce-scatter.5.cloned.1.call-done), channel_id=1, source_target_pairs={{10,0},{12,2},{14,4},{16,6},{18,8},{20,10},{22,12},{24,14},{26,16}... | collective-permute-start | bytes 98312 | tf_op jit(solution)/shard_map/ppermute | solution.py:15
  230.4 3.2 %collective-permute-start.22 = (f32[32,256]{1,0:T(8,128)}, f32[32,256]{1,0:T(8,128)S(1)}, u32[]{:S(2)}, u32[]{:S(2)}) collective-permute-start(f32[32,256]{1,0:T(8,128)} %reduce-scatter.5.cloned.1.call-done), channel_id=1, source_target_pairs={{28,0},{30,2},{0,4},{2,6},{4,8},{6,10},{8,12},{10,14},{12,16},{14,... | collective-permute-start | bytes 98312 | tf_op jit(solution)/shard_map/ppermute | solution.py:15
  233.5 6.6 %collective-permute-start.23 = (f32[32,256]{1,0:T(8,128)}, f32[32,256]{1,0:T(8,128)S(1)}, u32[]{:S(2)}, u32[]{:S(2)}) collective-permute-start(f32[32,256]{1,0:T(8,128)} %reduce-scatter.5.cloned.1.call-done), channel_id=1, source_target_pairs={{26,0},{28,2},{30,4},{0,6},{2,8},{4,10},{6,12},{8,14},{10,16},{12,... | collective-permute-start | bytes 98312 | tf_op jit(solution)/shard_map/ppermute | solution.py:15
  (17 other events, 66.7 us)
Sparse Core Ops, SparseCore 0:
  25.7 16.0 reduce-scatter.2
  196.9 12.6 reduce-scatter.4
where the time goes:
time: 318 us; the launch traced here: 316 us
  starting transfers between devices  59.5 us (19%)
  local copies, waits for them, and re-layouts  57 us (18%)
  blocking collectives  51.2 us (16%)
  matrix products  48.7 us (15%)
  loops' own time  41 us (13%)
  waiting for transfers between devices  31.1 us (10%)
  other arithmetic  13.9 us (4%)
  between operations  13.9 us (4%)
    ppermute x26, starting transfers between devices, from_behind(): return lax.ppermute(block, axis, route)  59.5 us
    another operation x2, loops' own time, couple_chips(): return lax.fori_loop(0, used_count, add_slot, start_value)  41 us
    psum x1, blocking collectives, on_device(): lax.psum(jnp.sum(first_pass * first_pass, axis=1), ('leaf', 'sub'))  39.2 us
    ppermute x26, waiting for transfers between devices, from_behind(): return lax.ppermute(block, axis, route)  20.7 us
    dynamic_slice x16, local copies, waits for them, and re-layouts, add_slot(): source = stacked[slot_place[slot_index]]  20.5 us
    dot_general x2, matrix products, apply_matrix(): jnp.einsum('clnp,lnpq->clq', source_values, kernels, precision=highest)  19.5 us
    dot_general x16, matrix products, add_slot(): jnp.dot(source, far_chip_blocks[slot_index], precision=highest, preferred...  19.2 us
    all_gather x2, blocking collectives, chip_level(): coupled = lax.all_gather(coupled_half, 'sub', axis=0, tiled=True)  11.9 us
  transfers between devices with their start and end apart: 28, of which 11 were waited for; matrix products, arithmetic and copies ran while one was open for 22% of the time, Pallas kernels for 0%

commit v1 on v0

--- a/solution.py
+++ b/solution.py
@@ -146,7 +146,7 @@
         far_chip_blocks,
         leaf_total,
     )
-    squares = lax.psum(jnp.sum(first_pass * first_pass, axis=1), ("leaf", "sub"))
+    squares = lax.psum(lax.psum(jnp.sum(first_pass * first_pass, axis=1), "leaf"), "sub")
     column_scale = lax.rsqrt(squares / point_total + epsilon)
     second = apply_matrix(
         first_pass * column_scale[:, None],

time: 318 us -> 318 us (level)
  blocking collectives: 51.2 us -> 46.2 us
  loops' own time: 41 us -> 44.2 us
    psum x1 -> x2, blocking collectives: 39.2 us -> 34.3 us  [the longest x1 24.8 us: on_device(): lax.psum(jnp.sum(first_pass * first_pass, axis=1), 'leaf')]
where the time goes in v1:
time: 318 us; the launch traced here: 316 us
  starting transfers between devices  60.9 us (19%)
  local copies, waits for them, and re-layouts  56.2 us (18%)
  matrix products  48.7 us (15%)
  blocking collectives  46.2 us (15%)
  loops' own time  44.2 us (14%)
  waiting for transfers between devices  32.6 us (10%)
  between operations  13.9 us (4%)
  other arithmetic  13.7 us (4%)
    ppermute x26, starting transfers between devices, from_behind(): return lax.ppermute(block, axis, route)  60.9 us
    another operation x2, loops' own time, couple_chips(): return lax.fori_loop(0, used_count, add_slot, start_value)  44.2 us
    psum x1, blocking collectives, on_device(): lax.psum(jnp.sum(first_pass * first_pass, axis=1), 'leaf')  24.8 us
    ppermute x26, waiting for transfers between devices, from_behind(): return lax.ppermute(block, axis, route)  20.7 us
    dynamic_slice x16, local copies, waits for them, and re-layouts, add_slot(): source = stacked[slot_place[slot_index]]  19.7 us
    dot_general x2, matrix products, apply_matrix(): jnp.einsum('clnp,lnpq->clq', source_values, kernels, precision=highest)  19.5 us
    dot_general x16, matrix products, add_slot(): jnp.dot(source, far_chip_blocks[slot_index], precision=highest, preferred...  19.2 us
    reduce_scatter x2, waiting for transfers between devices, chip_level(): halves = lax.psum_scatter(upward, 'sub', scatter_dimension=0, tiled=True)  12 us
  transfers between devices with their start and end apart: 28, of which 11 were waited for; matrix products, arithmetic and copies ran while one was open for 22% of the time, Pallas kernels for 0%

profile of v1, /device:TPU:5, one launch (start us, length us, event | category | flops | bytes accessed | tf_op | source)
XLA Modules:
  0.0 316.5 jit_solution(16943863681269111349)
XLA Ops:
  9.1 4.0 %gather_fusion.2 = f32[1024,64]{1,0:T(8,128)} fusion(f32[64,1024]{0,1:T(8,128)S(1)} %copy.43, s32[1024]{0:T(1024)S(1)} %get-tuple-element.107), kind=kCustom, calls=%fused_computation.6 | custom fusion | bytes 528384 | tf_op jit(solution)/shard_map/gather | solution.py:129
  13.2 2.1 fusion.58
  18.9 3.8 %gather_fusion = f32[1024,3]{1,0:T(8,128)S(1)} fusion(f32[3,1024]{0,1:T(8,128)} %copy.39, s32[1024]{0:T(1024)S(1)} %get-tuple-element.107), kind=kCustom, calls=%fused_computation.4 | custom fusion | bytes 28672 | tf_op jit(solution)/shard_map/gather | solution.py:130
  37.7 1.8 copy.42
  45.1 5.9 %collective-permute-start.6 = (f32[32,256]{1,0:T(8,128)}, f32[32,256]{1,0:T(8,128)S(1)}, u32[]{:S(2)}, u32[]{:S(2)}) collective-permute-start(f32[32,256]{1,0:T(8,128)} %reduce-scatter.3.cloned.1.call-done), channel_id=1, source_target_pairs={{4,0},{6,2},{8,4},{10,6},{12,8},{14,10},{16,12},{18,14},{20,16},{2... | collective-permute-start | bytes 98312 | tf_op jit(solution)/shard_map/ppermute | solution.py:15
  54.8 10.9 %collective-permute-start.7 = (f32[32,256]{1,0:T(8,128)}, f32[32,256]{1,0:T(8,128)S(1)}, u32[]{:S(2)}, u32[]{:S(2)}) collective-permute-start(f32[32,256]{1,0:T(8,128)} %reduce-scatter.3.cloned.1.call-done), channel_id=1, source_target_pairs={{6,0},{8,2},{10,4},{12,6},{14,8},{16,10},{18,12},{20,14},{22,16},{... | collective-permute-start | bytes 98312 | tf_op jit(solution)/shard_map/ppermute | solution.py:15
  67.3 3.2 %collective-permute-done.8 = f32[32,256]{1,0:T(8,128)S(1)} collective-permute-done((f32[32,256]{1,0:T(8,128)}, f32[32,256]{1,0:T(8,128)S(1)}, u32[]{:S(2)}, u32[]{:S(2)}) %collective-permute-start.8) | collective-permute-done | bytes 32800 | tf_op jit(solution)/shard_map/ppermute | solution.py:15
  70.5 5.1 %collective-permute-start.9 = (f32[32,256]{1,0:T(8,128)}, f32[32,256]{1,0:T(8,128)S(1)}, u32[]{:S(2)}, u32[]{:S(2)}) collective-permute-start(f32[32,256]{1,0:T(8,128)} %reduce-scatter.3.cloned.1.call-done), channel_id=1, source_target_pairs={{10,0},{12,2},{14,4},{16,6},{18,8},{20,10},{22,12},{24,14},{26,16}... | collective-permute-start | bytes 98312 | tf_op jit(solution)/shard_map/ppermute | solution.py:15
  77.0 1.8 collective-permute-start.10
  80.3 2.5 collective-permute-start.11
  82.7 3.7 %collective-permute-done.11 = f32[32,256]{1,0:T(8,128)S(1)} collective-permute-done((f32[32,256]{1,0:T(8,128)}, f32[32,256]{1,0:T(8,128)S(1)}, u32[]{:S(2)}, u32[]{:S(2)}) %collective-permute-start.11) | collective-permute-done | bytes 32800 | tf_op jit(solution)/shard_map/ppermute | solution.py:15
  87.1 41.1 %while.20 = (s32[]{:T(128)}, f32[32,256]{1,0:T(8,128)S(1)}, s32[]{:T(128)}, s32[8]{0:T(128)}, f32[8,32,256]{2,1,0:T(8,128)}, /*index=5*/f32[8,256,256]{2,1,0:T(8,128)}, s32[]{:T(128)}, s32[]{:T(128)}, s32[]{:T(128)}) while((s32[]{:T(128)}, f32[32,256]{1,0:T(8,128)S(1)}, s32[]{:T(128)}, s32[8]{0:T(128)}, f32[8,32,256]{2,1,0:T(8,128)}, ...), condition=%wide.region_3.6_spmd, body=%wide.region_2.5_spmd.sunk | while | flops 25174024 | bytes 360637 | solution.py:50
  128.3 3.8 %all_gather.6 = f32[64,256]{1,0:T(8,128)S(1)} all-gather(f32[32,256]{1,0:T(8,128)S(1)} %get-tuple-element.73), channel_id=1, replica_groups=mesh['leaf'=16,'sub'=2] {'sub'}, dimensions={0}, use_global_device_ids=true | all-gather | bytes 98304 | tf_op jit(solution)/shard_map/all_gather | solution.py:69
  132.7 2.4 pad_maximum_fusion
  135.2 3.6 %gather_fusion.3 = f32[8,64,512]{1,2,0:T(8,128)} fusion(f32[64,6,512]{0,2,1:T(8,128)} %bitcast.168, s32[1024]{0:T(1024)} %pad_clamp_fusion.1), kind=kCustom, calls=%fused_computation.clone | custom fusion | bytes 2097184 | tf_op jit(solution)/shard_map/jit(_take)/gather | solution.py:89
  138.8 3.2 %copy.44 = f32[8,64,512]{2,1,0:T(8,128)} copy(f32[8,64,512]{1,2,0:T(8,128)} %gather_fusion.3) | data formatting | bytes 2097152 | tf_op jit(solution)/shard_map/jit(_take)/gather | solution.py:89
  142.0 9.7 %fusion.26 = f32[64,2,512]{2,0,1:T(8,128)S(1)} fusion(f32[2,512]{1,0:T(2,128)S(1)} %copy-done.13, f32[2,4,512]{2,1,0:T(4,128)S(1)} %copy-done.5, f32[2,512]{1,0:T(2,128)S(1)} %copy-done.11, f32[2,4,512]{2,1,0:T(4,128)S(1)} %copy-done.7, f32[2,512]{1,0:T(2,128)S(1)} %copy-done.9, f32[2,4,512]{2,1,0:T(4,128)S(1)} %bitcast.184, ...), kind=kOutput, calls=%fused_computation.38 | convolution fusion | flops 1629749248 | bytes 1372168 | tf_op jit(solution)/shard_map/clnp,lnpq->clq/dot_general | solution.py:90
  153.0 24.8 %psum.14 = f32[64]{0:T(128)S(1)} all-reduce(f32[64]{0:T(128)S(1)} %get-tuple-element.109), channel_id=1, replica_groups=mesh['leaf'=16,'sub'=2] {'leaf'}, use_global_device_ids=true, to_apply=%region_5.8 | all-reduce | flops 64 | bytes 512 | tf_op jit(solution)/shard_map/psum | solution.py:149
  177.8 9.5 %psum.15 = f32[64]{0:T(128)S(1)} all-reduce(f32[64]{0:T(128)S(1)} %psum.14), channel_id=1, replica_groups=mesh['leaf'=16,'sub'=2] {'sub'}, use_global_device_ids=true, to_apply=%region_6.9 | all-reduce | flops 64 | bytes 512 | tf_op jit(solution)/shard_map/psum | solution.py:149
  190.9 3.7 %collective-permute-start.15 = (f32[64,1024]{1,0:T(8,128)}, f32[64,1024]{1,0:T(8,128)}, u32[]{:S(2)}, u32[]{:S(2)}) collective-permute-start(f32[64,1024]{1,0:T(8,128)} %broadcast_multiply_fusion), channel_id=1, source_target_pairs={{1,0},{2,1},{3,2},{4,3},{5,4},{6,5},{7,6},{8,7},{9,8},{10,9},{11,1... | collective-permute-start | bytes 786440 | tf_op jit(solution)/shard_map/ppermute | solution.py:15
  198.0 11.9 %reduce-scatter.5.cloned.1.call-done = f32[32,256]{1,0:T(8,128)} async-done(((f32[64,256]{1,0:T(8,128)}), f32[32,256]{1,0:T(8,128)}) %reduce-scatter.5.cloned.1.call-update) | async-done | bytes 32784 | tf_op jit(solution)/shard_map/reduce_scatter | solution.py:66
  210.7 2.4 collective-permute-start.25
  214.3 5.3 %collective-permute-start.19 = (f32[32,256]{1,0:T(8,128)}, f32[32,256]{1,0:T(8,128)S(1)}, u32[]{:S(2)}, u32[]{:S(2)}) collective-permute-start(f32[32,256]{1,0:T(8,128)} %reduce-scatter.5.cloned.1.call-done), channel_id=1, source_target_pairs={{6,0},{8,2},{10,4},{12,6},{14,8},{16,10},{18,12},{20,14},{22,16},{... | collective-permute-start | bytes 98312 | tf_op jit(solution)/shard_map/ppermute | solution.py:15
  220.9 4.5 %collective-permute-start.20 = (f32[32,256]{1,0:T(8,128)}, f32[32,256]{1,0:T(8,128)S(1)}, u32[]{:S(2)}, u32[]{:S(2)}) collective-permute-start(f32[32,256]{1,0:T(8,128)} %reduce-scatter.5.cloned.1.call-done), channel_id=1, source_target_pairs={{8,0},{10,2},{12,4},{14,6},{16,8},{18,10},{20,12},{22,14},{24,16},... | collective-permute-start | bytes 98312 | tf_op jit(solution)/shard_map/ppermute | solution.py:15
  226.7 2.7 collective-permute-start.21
  230.7 1.8 collective-permute-start.22
  233.9 2.4 collective-permute-start.23
  236.2 4.2 %collective-permute-done.23 = f32[32,256]{1,0:T(8,128)S(1)} collective-permute-done((f32[32,256]{1,0:T(8,128)}, f32[32,256]{1,0:T(8,128)S(1)}, u32[]{:S(2)}, u32[]{:S(2)}) %collective-permute-start.23) | collective-permute-done | bytes 32800 | tf_op jit(solution)/shard_map/ppermute | solution.py:15
  240.5 42.0 %while.21 = (s32[]{:T(128)}, f32[32,256]{1,0:T(8,128)S(1)}, s32[]{:T(128)}, s32[8]{0:T(128)}, f32[8,32,256]{2,1,0:T(8,128)S(1)}, /*index=5*/f32[8,256,256]{2,1,0:T(8,128)}, s32[]{:T(128)}, s32[]{:T(128)}, s32[]{:T(128)}) while((s32[]{:T(128)}, f32[32,256]{1,0:T(8,128)S(1)}, s32[]{:T(128)}, s32[8]{0:T(128)}, f32[8,32,256]{2,1,0:T(8,128)S(1)}, ...), condition=%wide.region_9.12_spmd, body=%wide.region_8.11_spmd.sunk | while | flops 25174024 | bytes 360637 | solution.py:50
  282.5 8.1 %all_gather.7 = f32[64,256]{1,0:T(8,128)S(1)} all-gather(f32[32,256]{1,0:T(8,128)S(1)} %get-tuple-element.74), channel_id=1, replica_groups=mesh['leaf'=16,'sub'=2] {'sub'}, dimensions={0}, use_global_device_ids=true | all-gather | bytes 98304 | tf_op jit(solution)/shard_map/all_gather | solution.py:69
  294.3 9.7 %fusion.27 = f32[64,2,512]{2,0,1:T(8,128)S(1)} fusion(f32[2,512]{1,0:T(2,128)S(1)} %copy-done.14, f32[2,4,512]{2,1,0:T(4,128)S(1)} %copy-done.6, f32[2,512]{1,0:T(2,128)S(1)} %copy-done.12, f32[2,4,512]{2,1,0:T(4,128)S(1)} %copy-done.8, f32[2,512]{1,0:T(2,128)S(1)} %copy-done.10, f32[2,4,512]{2,1,0:T(4,128)S(1)} %bitcast.185, ...), kind=kOutput, calls=%fused_computation.39 | convolution fusion | flops 1629749248 | bytes 1372168 | tf_op jit(solution)/shard_map/clnp,lnpq->clq/dot_general | solution.py:90
  305.4 3.3 %scatter_custom_fusion = f32[64,1024]{0,1:T(8,128)S(1)} fusion(s32[1024]{0:T(1024)} %get-tuple-element.108, f32[1024,64]{1,0:T(8,128)S(1)} %copy.49, f32[]{:T(128)} %constant.109.clone.1), kind=kCustom, calls=%fused_computation.71 | custom fusion | bytes 262656 | tf_op jit(solution)/shard_map/scatter | solution.py:163
  (183 shorter events, 96.5 us)
Async XLA Ops:
  6.5 44.5 %copy-start = (f32[4,256,256]{2,1,0:T(8,128)S(1)}, f32[4,256,256]{2,1,0:T(8,128)}, u32[]{:S(2)}) copy-start(f32[4,256,256]{2,1,0:T(8,128)} %param.26) | copy-start | bytes 3145732
  6.5 38.6 %reduce-scatter.3.cloned.1.call-start = ((), (), s32[]{:S(2)}) async-start(), calls=%async_computation.2 | async-start | bytes 98304 | tf_op jit(solution)/shard_map/reduce_scatter | solution.py:66
  13.2 16.3 %copy-start.19 = (s32[1,8]{1,0:T(1,128)S(1)}, s32[1,8]{1,0:T(1,128)}, u32[]{:S(2)}) copy-start(s32[1,8]{1,0:T(1,128)} %param.23) | copy-start | bytes 100
  13.2 16.8 %copy-start.17 = (s32[2,4]{1,0:T(2,128)S(1)}, s32[2,4]{1,0:T(2,128)}, u32[]{:S(2)}) copy-start(s32[2,4]{1,0:T(2,128)} %param.21) | copy-start | bytes 100
  15.3 28.4 %collective-permute-start.5 = (f32[2,64,256]{2,1,0:T(8,128)S(1)}, f32[2,64,256]{2,1,0:T(8,128)S(1)}, u32[]{:S(2)}, u32[]{:S(2)}) collective-permute-start(f32[2,64,256]{2,1,0:T(8,128)S(1)} %fusion.58), channel_id=1, source_target_pairs={{1,0},{2,1},{3,2},{4,3},{5,4},{6,5},{7,6},{8,7},{9,8},{10,9},{11,1... | collective-permute-start | bytes 393224 | tf_op jit(solution)/shard_map/ppermute | solution.py:15
  16.0 27.7 %collective-permute-start.4 = (f32[2,64,256]{2,1,0:T(8,128)S(1)}, f32[2,64,256]{2,1,0:T(8,128)S(1)}, u32[]{:S(2)}, u32[]{:S(2)}) collective-permute-start(f32[2,64,256]{2,1,0:T(8,128)S(1)} %fusion.58), channel_id=1, source_target_pairs={{31,0},{0,1},{1,2},{2,3},{3,4},{4,5},{5,6},{6,7},{7,8},{8,9},{9,10... | collective-permute-start | bytes 393224 | tf_op jit(solution)/shard_map/ppermute | solution.py:15
  22.8 13.8 %collective-permute-start.1 = (f32[3,1024]{0,1:T(8,128)S(1)}, f32[3,1024]{0,1:T(8,128)}, u32[]{:S(2)}, u32[]{:S(2)}) collective-permute-start(f32[3,1024]{0,1:T(8,128)S(1)} %bitcast.164), channel_id=1, source_target_pairs={{1,0},{2,1},{3,2},{4,3},{5,4},{6,5},{7,6},{8,7},{9,8},{10,9},{11,1... | collective-permute-start | bytes 36872 | tf_op jit(solution)/shard_map/ppermute | solution.py:15
  22.8 16.7 %collective-permute-start = (f32[3,1024]{0,1:T(8,128)S(1)}, f32[3,1024]{0,1:T(8,128)}, u32[]{:S(2)}, u32[]{:S(2)}) collective-permute-start(f32[3,1024]{0,1:T(8,128)S(1)} %bitcast.165), channel_id=1, source_target_pairs={{31,0},{0,1},{1,2},{2,3},{3,4},{4,5},{5,6},{6,7},{7,8},{8,9},{9,10... | collective-permute-start | bytes 36872 | tf_op jit(solution)/shard_map/ppermute | solution.py:15
  25.6 184.3 %reduce-scatter.5.cloned.1.call-start = ((), (), s32[]{:S(2)}) async-start(), calls=%async_computation.3 | async-start | bytes 98304 | tf_op jit(solution)/shard_map/reduce_scatter | solution.py:66
  25.7 107.0 %collective-permute-start.3 = (f32[64,1024]{0,1:T(8,128)}, f32[64,1024]{0,1:T(8,128)}, u32[]{:S(2)}, u32[]{:S(2)}) collective-permute-start(f32[64,1024]{0,1:T(8,128)} %bitcast.171), channel_id=1, source_target_pairs={{1,0},{2,1},{3,2},{4,3},{5,4},{6,5},{7,6},{8,7},{9,8},{10,9},{11,1... | collective-permute-start | bytes 786440 | tf_op jit(solution)/shard_map/ppermute | solution.py:15
  36.6 96.1 %collective-permute-start.2 = (f32[64,1024]{0,1:T(8,128)}, f32[64,1024]{0,1:T(8,128)}, u32[]{:S(2)}, u32[]{:S(2)}) collective-permute-start(f32[64,1024]{0,1:T(8,128)} %bitcast.172), channel_id=1, source_target_pairs={{31,0},{0,1},{1,2},{2,3},{3,4},{4,5},{5,6},{6,7},{7,8},{8,9},{9,10... | collective-permute-start | bytes 786440 | tf_op jit(solution)/shard_map/ppermute | solution.py:15
  45.1 9.7 %collective-permute-start.6 = (f32[32,256]{1,0:T(8,128)}, f32[32,256]{1,0:T(8,128)S(1)}, u32[]{:S(2)}, u32[]{:S(2)}) collective-permute-start(f32[32,256]{1,0:T(8,128)} %reduce-scatter.3.cloned.1.call-done), channel_id=1, source_target_pairs={{4,0},{6,2},{8,4},{10,6},{12,8},{14,10},{16,12},{18,14},{20,16},{2... | collective-permute-start | bytes 98312 | tf_op jit(solution)/shard_map/ppermute | solution.py:15
  51.8 80.9 %copy-start.3 = (f32[1024,64]{1,0:T(8,128)S(1)}, f32[1024,64]{1,0:T(8,128)}, u32[]{:S(2)}) copy-start(f32[1024,64]{1,0:T(8,128)} %gather_fusion.2) | copy-start | bytes 786436
  51.8 34.6 %collective-permute-start.13 = (f32[32,256]{1,0:T(8,128)}, f32[32,256]{1,0:T(8,128)S(1)}, u32[]{:S(2)}, u32[]{:S(2)}) collective-permute-start(f32[32,256]{1,0:T(8,128)} %reduce-scatter.3.cloned.1.call-done), channel_id=1, source_target_pairs={{22,0},{24,2},{26,4},{28,6},{30,8},{0,10},{2,12},{4,14},{6,16},{8,... | collective-permute-start | bytes 98312 | tf_op jit(solution)/shard_map/ppermute | solution.py:15
  53.5 32.9 %collective-permute-start.12 = (f32[32,256]{1,0:T(8,128)}, f32[32,256]{1,0:T(8,128)S(1)}, u32[]{:S(2)}, u32[]{:S(2)}) collective-permute-start(f32[32,256]{1,0:T(8,128)} %reduce-scatter.3.cloned.1.call-done), channel_id=1, source_target_pairs={{24,0},{26,2},{28,4},{30,6},{0,8},{2,10},{4,12},{6,14},{8,16},{10,... | collective-permute-start | bytes 98312 | tf_op jit(solution)/shard_map/ppermute | solution.py:15
  54.8 12.3 %collective-permute-start.7 = (f32[32,256]{1,0:T(8,128)}, f32[32,256]{1,0:T(8,128)S(1)}, u32[]{:S(2)}, u32[]{:S(2)}) collective-permute-start(f32[32,256]{1,0:T(8,128)} %reduce-scatter.3.cloned.1.call-done), channel_id=1, source_target_pairs={{6,0},{8,2},{10,4},{12,6},{14,8},{16,10},{18,12},{20,14},{22,16},{... | collective-permute-start | bytes 98312 | tf_op jit(solution)/shard_map/ppermute | solution.py:15
  67.1 3.4 %collective-permute-start.8 = (f32[32,256]{1,0:T(8,128)}, f32[32,256]{1,0:T(8,128)S(1)}, u32[]{:S(2)}, u32[]{:S(2)}) collective-permute-start(f32[32,256]{1,0:T(8,128)} %reduce-scatter.3.cloned.1.call-done), channel_id=1, source_target_pairs={{8,0},{10,2},{12,4},{14,6},{16,8},{18,10},{20,12},{22,14},{24,16},... | collective-permute-start | bytes 98312 | tf_op jit(solution)/shard_map/ppermute | solution.py:15
  70.5 6.4 %collective-permute-start.9 = (f32[32,256]{1,0:T(8,128)}, f32[32,256]{1,0:T(8,128)S(1)}, u32[]{:S(2)}, u32[]{:S(2)}) collective-permute-start(f32[32,256]{1,0:T(8,128)} %reduce-scatter.3.cloned.1.call-done), channel_id=1, source_target_pairs={{10,0},{12,2},{14,4},{16,6},{18,8},{20,10},{22,12},{24,14},{26,16}... | collective-permute-start | bytes 98312 | tf_op jit(solution)/shard_map/ppermute | solution.py:15
  77.0 3.3 %collective-permute-start.10 = (f32[32,256]{1,0:T(8,128)}, f32[32,256]{1,0:T(8,128)S(1)}, u32[]{:S(2)}, u32[]{:S(2)}) collective-permute-start(f32[32,256]{1,0:T(8,128)} %reduce-scatter.3.cloned.1.call-done), channel_id=1, source_target_pairs={{28,0},{30,2},{0,4},{2,6},{4,8},{6,10},{8,12},{10,14},{12,16},{14,... | collective-permute-start | bytes 98312 | tf_op jit(solution)/shard_map/ppermute | solution.py:15
  80.3 6.1 %collective-permute-start.11 = (f32[32,256]{1,0:T(8,128)}, f32[32,256]{1,0:T(8,128)S(1)}, u32[]{:S(2)}, u32[]{:S(2)}) collective-permute-start(f32[32,256]{1,0:T(8,128)} %reduce-scatter.3.cloned.1.call-done), channel_id=1, source_target_pairs={{26,0},{28,2},{30,4},{0,6},{2,8},{4,10},{6,12},{8,14},{10,16},{12,... | collective-permute-start | bytes 98312 | tf_op jit(solution)/shard_map/ppermute | solution.py:15
  188.0 7.6 %collective-permute-start.17 = (f32[2,64,256]{2,1,0:T(8,128)S(1)}, f32[2,64,256]{2,1,0:T(8,128)S(1)}, u32[]{:S(2)}, u32[]{:S(2)}) collective-permute-start(f32[2,64,256]{2,1,0:T(8,128)S(1)} %fusion.41), channel_id=1, source_target_pairs={{1,0},{2,1},{3,2},{4,3},{5,4},{6,5},{7,6},{8,7},{9,8},{10,9},{11,1... | collective-permute-start | bytes 393224 | tf_op jit(solution)/shard_map/ppermute | solution.py:15
  188.4 7.2 %collective-permute-start.16 = (f32[2,64,256]{2,1,0:T(8,128)S(1)}, f32[2,64,256]{2,1,0:T(8,128)}, u32[]{:S(2)}, u32[]{:S(2)}) collective-permute-start(f32[2,64,256]{2,1,0:T(8,128)S(1)} %fusion.41), channel_id=1, source_target_pairs={{31,0},{0,1},{1,2},{2,3},{3,4},{4,5},{5,6},{6,7},{7,8},{8,9},{9,10... | collective-permute-start | bytes 393224 | tf_op jit(solution)/shard_map/ppermute | solution.py:15
  190.9 100.3 %collective-permute-start.15 = (f32[64,1024]{1,0:T(8,128)}, f32[64,1024]{1,0:T(8,128)}, u32[]{:S(2)}, u32[]{:S(2)}) collective-permute-start(f32[64,1024]{1,0:T(8,128)} %broadcast_multiply_fusion), channel_id=1, source_target_pairs={{1,0},{2,1},{3,2},{4,3},{5,4},{6,5},{7,6},{8,7},{9,8},{10,9},{11,1... | collective-permute-start | bytes 786440 | tf_op jit(solution)/shard_map/ppermute | solution.py:15
  194.6 96.6 %collective-permute-start.14 = (f32[64,1024]{1,0:T(8,128)}, f32[64,1024]{1,0:T(8,128)}, u32[]{:S(2)}, u32[]{:S(2)}) collective-permute-start(f32[64,1024]{1,0:T(8,128)} %broadcast_multiply_fusion), channel_id=1, source_target_pairs={{31,0},{0,1},{1,2},{2,3},{3,4},{4,5},{5,6},{6,7},{7,8},{8,9},{9,10... | collective-permute-start | bytes 786440 | tf_op jit(solution)/shard_map/ppermute | solution.py:15
  209.9 4.4 %collective-permute-start.18 = (f32[32,256]{1,0:T(8,128)}, f32[32,256]{1,0:T(8,128)S(1)}, u32[]{:S(2)}, u32[]{:S(2)}) collective-permute-start(f32[32,256]{1,0:T(8,128)} %reduce-scatter.5.cloned.1.call-done), channel_id=1, source_target_pairs={{4,0},{6,2},{8,4},{10,6},{12,8},{14,10},{16,12},{18,14},{20,16},{2... | collective-permute-start | bytes 98312 | tf_op jit(solution)/shard_map/ppermute | solution.py:15
  210.7 29.8 %collective-permute-start.25 = (f32[32,256]{1,0:T(8,128)}, f32[32,256]{1,0:T(8,128)S(1)}, u32[]{:S(2)}, u32[]{:S(2)}) collective-permute-start(f32[32,256]{1,0:T(8,128)} %reduce-scatter.5.cloned.1.call-done), channel_id=1, source_target_pairs={{22,0},{24,2},{26,4},{28,6},{30,8},{0,10},{2,12},{4,14},{6,16},{8,... | collective-permute-start | bytes 98312 | tf_op jit(solution)/shard_map/ppermute | solution.py:15
  213.1 27.4 %collective-permute-start.24 = (f32[32,256]{1,0:T(8,128)}, f32[32,256]{1,0:T(8,128)S(1)}, u32[]{:S(2)}, u32[]{:S(2)}) collective-permute-start(f32[32,256]{1,0:T(8,128)} %reduce-scatter.5.cloned.1.call-done), channel_id=1, source_target_pairs={{24,0},{26,2},{28,4},{30,6},{0,8},{2,10},{4,12},{6,14},{8,16},{10,... | collective-permute-start | bytes 98312 | tf_op jit(solution)/shard_map/ppermute | solution.py:15
  214.3 6.6 %collective-permute-start.19 = (f32[32,256]{1,0:T(8,128)}, f32[32,256]{1,0:T(8,128)S(1)}, u32[]{:S(2)}, u32[]{:S(2)}) collective-permute-start(f32[32,256]{1,0:T(8,128)} %reduce-scatter.5.cloned.1.call-done), channel_id=1, source_target_pairs={{6,0},{8,2},{10,4},{12,6},{14,8},{16,10},{18,12},{20,14},{22,16},{... | collective-permute-start | bytes 98312 | tf_op jit(solution)/shard_map/ppermute | solution.py:15
  220.9 5.8 %collective-permute-start.20 = (f32[32,256]{1,0:T(8,128)}, f32[32,256]{1,0:T(8,128)S(1)}, u32[]{:S(2)}, u32[]{:S(2)}) collective-permute-start(f32[32,256]{1,0:T(8,128)} %reduce-scatter.5.cloned.1.call-done), channel_id=1, source_target_pairs={{8,0},{10,2},{12,4},{14,6},{16,8},{18,10},{20,12},{22,14},{24,16},... | collective-permute-start | bytes 98312 | tf_op jit(solution)/shard_map/ppermute | solution.py:15
  226.7 4.0 %collective-permute-start.21 = (f32[32,256]{1,0:T(8,128)}, f32[32,256]{1,0:T(8,128)S(1)}, u32[]{:S(2)}, u32[]{:S(2)}) collective-permute-start(f32[32,256]{1,0:T(8,128)} %reduce-scatter.5.cloned.1.call-done), channel_id=1, source_target_pairs={{10,0},{12,2},{14,4},{16,6},{18,8},{20,10},{22,12},{24,14},{26,16}... | collective-permute-start | bytes 98312 | tf_op jit(solution)/shard_map/ppermute | solution.py:15
  230.7 3.2 %collective-permute-start.22 = (f32[32,256]{1,0:T(8,128)}, f32[32,256]{1,0:T(8,128)S(1)}, u32[]{:S(2)}, u32[]{:S(2)}) collective-permute-start(f32[32,256]{1,0:T(8,128)} %reduce-scatter.5.cloned.1.call-done), channel_id=1, source_target_pairs={{28,0},{30,2},{0,4},{2,6},{4,8},{6,10},{8,12},{10,14},{12,16},{14,... | collective-permute-start | bytes 98312 | tf_op jit(solution)/shard_map/ppermute | solution.py:15
  233.9 6.6 %collective-permute-start.23 = (f32[32,256]{1,0:T(8,128)}, f32[32,256]{1,0:T(8,128)S(1)}, u32[]{:S(2)}, u32[]{:S(2)}) collective-permute-start(f32[32,256]{1,0:T(8,128)} %reduce-scatter.5.cloned.1.call-done), channel_id=1, source_target_pairs={{26,0},{28,2},{30,4},{0,6},{2,8},{4,10},{6,12},{8,14},{10,16},{12,... | collective-permute-start | bytes 98312 | tf_op jit(solution)/shard_map/ppermute | solution.py:15
  (17 other events, 66.8 us)
Sparse Core Ops, SparseCore 0:
  25.7 16.0 reduce-scatter.2
  195.8 14.0 reduce-scatter.4
